TPU v7x, 32 devices: a whole 2x2x4 slice. The times are simulated.
32 devices in a mesh: beam: 8 (over y, x, core), freq: 4 (over z).
Axes of the slice: x: 2, y: 2, z: 4, core: 2. Of those that a mesh axis runs over, the one named last changes fastest.
Arguments:
- intensity: bfloat16 [8, 16384, 256], P(None, ('freq', 'beam')), may hold values from -600 to 600, as said below
- channel_mask: int32 [16384], P('freq'), may hold values 0 or 1
- box_widths: int32 [9], replicated, may hold values from 1 to 64
Outputs:
- snr_peak: float32 [8, 4096], P('beam', 'freq')
Inputs may be any that keep to these rules, and one draw needn't show every extreme that they name: `intensity`: filterbank intensities of every beam and channel, of any sign.
All inputs are finite; a program needn't handle non-finite values. No bound on the sum of `channel_mask` on one device may be relied on, other than what follows from the above.
Results may differ from a plain program's by a relative error of at most 0.002.
Values may be sent and summed in bfloat16 or wider, within the bound.
A program may use at most 64 MiB of HBM per device.

v0:
```python
import functools

import jax
import jax.numpy as jnp
from jax import lax
from jax.experimental import pallas as pl
from jax.experimental.pallas import tpu as pltpu
from jax.sharding import PartitionSpec as P

CHANS = 16384
NDM = 4096
LANE_ROWS = 8

epsilon = 1e-05


def reverse_bits(number, count):
    result = 0
    for _ in range(count):
        result = result << 1 | number & 1
        number >>= 1
    return result


def rolled(block, amount):
    samples = block.shape[-1]
    if isinstance(amount, int):
        amount = amount % samples
        return block if amount == 0 else pltpu.roll(block, samples - amount, block.ndim - 1)
    return pltpu.roll(block, (samples - 1) & (samples - amount), block.ndim - 1)


def lane_index(shape):
    return lax.broadcasted_iota(jnp.int32, shape, len(shape) - 1)


def earlier(block, amount):
    samples = block.shape[-1]
    if isinstance(amount, int) and amount == 0:
        return block
    return jnp.where(lane_index(block.shape) < samples - amount, rolled(block, amount), 0.0)


def entry_kernel(row_total, place_ref, x_ref, mask_ref, out_ref):
    rows, beams, bands, samples = out_ref.shape
    width = x_ref.shape[1]
    group = width // (bands * rows)
    total = jnp.zeros((width, samples), jnp.float32)
    squares = jnp.zeros((width, samples), jnp.float32)
    for beam in range(beams):
        wide = x_ref[beam].astype(jnp.float32)
        total = total + wide
        squares = squares + wide * wide
    channel_mean = jnp.sum(total, axis=1, keepdims=True) / row_total
    channel_var = jnp.sum(squares, axis=1, keepdims=True) / row_total - channel_mean * channel_mean
    channel_scale = lax.rsqrt(channel_var + epsilon)
    out_row = lax.broadcasted_iota(jnp.int32, (rows * bands, width), 0)
    channel = lax.broadcasted_iota(jnp.int32, (rows * bands, width), 1)
    wanted = (out_row % bands) * rows + out_row // bands
    clean = mask_ref[pl.ds(place_ref[0], 1), :].astype(jnp.float32)
    chosen = jnp.where(channel // group == wanted, clean, 0.0).astype(jnp.bfloat16)
    for beam in range(beams):
        wide = x_ref[beam].astype(jnp.float32)
        normed = ((wide - channel_mean) * channel_scale).astype(jnp.bfloat16)
        sums = jnp.dot(chosen, normed, preferred_element_type=jnp.float32)
        tree = [[sums[i * bands:(i + 1) * bands]] for i in range(rows)]
        while len(tree) > 1:
            merged = []
            for low, high in zip(tree[0::2], tree[1::2]):
                merged.append(
                    [low[m // 2] + earlier(high[m // 2], (m + 1) // 2) for m in range(2 * len(low))]
                )
            tree = merged
        for number, row in enumerate(tree[0]):
            out_ref[number, beam] = row.astype(jnp.bfloat16)


def entry_rows(intensity, mask_rows, place, rows):
    beams, width, samples = intensity.shape
    bands = width * NDM // (CHANS * rows)
    chunks = 2 if bands % 32 == 0 else 1
    return pl.pallas_call(
        functools.partial(entry_kernel, float(beams * samples)),
        grid_spec=pltpu.PrefetchScalarGridSpec(
            num_scalar_prefetch=1,
            grid=(chunks,),
            in_specs=[
                pl.BlockSpec((beams, width // chunks, samples), lambda c, p: (0, c, 0)),
                pl.BlockSpec((mask_rows.shape[0], width // chunks), lambda c, p: (0, c)),
            ],
            out_specs=pl.BlockSpec((rows, beams, bands // chunks, samples), lambda c, p: (0, 0, c, 0)),
        ),
        out_shape=jax.ShapeDtypeStruct((rows, beams, bands, samples), jnp.bfloat16),
    )(place, intensity, mask_rows)


def trial_kernel(place_ref, widths_ref, x_ref, out_ref, first, even, odd, series, boxes):
    total, samples = x_ref.shape[1:]
    tiles = total // LANE_ROWS
    tile_bits = tiles.bit_length() - 1
    block = place_ref[0]
    for high in range(LANE_ROWS):
        spot = reverse_bits(high, LANE_ROWS.bit_length() - 1)
        for part in range(samples // 128):
            first[part, spot * tiles:(spot + 1) * tiles] = x_ref[
                0, high * tiles:(high + 1) * tiles, part * 128:(part + 1) * 128
            ].astype(jnp.float32)
    for tile in range(tiles):
        for part in range(samples // 128):
            even[reverse_bits(tile, tile_bits), :, part * 128:(part + 1) * 128] = first[
                part, pl.ds(tile, LANE_ROWS, stride=tiles)
            ]

    source, target = even, odd
    count = 1
    while count < tiles:
        half = tiles // count // 2

        def merge(j, source=source, target=target, count=count, half=half):
            low = source[pl.ds(j * 2 * half, half)].reshape(half * LANE_ROWS, samples)
            high = source[pl.ds(j * 2 * half + half, half)].reshape(half * LANE_ROWS, samples)
            moved = earlier(high, block * count + j)
            target[pl.ds(2 * j * half, half)] = (low + moved).reshape(half, LANE_ROWS, samples)
            target[pl.ds((2 * j + 1) * half, half)] = (low + earlier(moved, 1)).reshape(half, LANE_ROWS, samples)

        if count <= 8:
            for j in range(count):
                merge(j)
        else:
            def step(i, carry, merge=merge):
                for k in range(8):
                    merge(i * 8 + k)
                return carry
            lax.fori_loop(0, count // 8, step, 0)
        source, target = target, source
        count = count * 2

    shape = (LANE_ROWS, samples)
    lane = lane_index(shape)
    spot = lax.broadcasted_iota(jnp.int32, shape, 0)
    bit_high, bit_mid, bit_low = spot >> 2 & 1, spot >> 1 & 1, spot & 1

    def final_rows(j):
        tree = source[j]
        row = block * tiles + j
        other = pltpu.roll(tree, 4, 0)
        low = jnp.where(bit_high == 0, tree, other)
        high = rolled(jnp.where(bit_high == 0, other, tree), row)
        high = jnp.where(bit_high == 1, rolled(high, 1), high)
        tree = low + jnp.where(lane + (row + bit_high) < samples, high, 0.0)
        low = jnp.where(bit_mid == 0, tree, pltpu.roll(tree, 2, 0))
        high = rolled(jnp.where(bit_mid == 0, pltpu.roll(tree, LANE_ROWS - 2, 0), tree), 2 * row)
        high = jnp.where(bit_high == 1, rolled(high, 1), high)
        high = jnp.where(bit_mid == 1, rolled(high, 1), high)
        tree = low + jnp.where(lane + (2 * row + bit_high + bit_mid) < samples, high, 0.0)
        low = jnp.where(bit_low == 0, tree, pltpu.roll(tree, 1, 0))
        high = rolled(jnp.where(bit_low == 0, pltpu.roll(tree, LANE_ROWS - 1, 0), tree), 4 * row)
        high = jnp.where(bit_high == 1, rolled(high, 2), high)
        high = jnp.where(bit_mid == 1, rolled(high, 1), high)
        high = jnp.where(bit_low == 1, rolled(high, 1), high)
        return low + jnp.where(lane + (4 * row + 2 * bit_high + bit_mid + bit_low) < samples, high, 0.0)

    def finish(i, carry):
        for k in range(4):
            pair = i * 4 + k
            rows = jnp.concatenate([final_rows(2 * pair), final_rows(2 * pair + 1)], axis=0)
            coarse = rows.astype(jnp.bfloat16)
            place = pl.ds(pl.multiple_of(pair * 16, 16), 16)
            series[place, :samples] = coarse
            series[place, samples:] = (rows - coarse.astype(jnp.float32)).astype(jnp.bfloat16)
        return carry

    lax.fori_loop(0, tiles // 8, finish, 0)

    start = lax.broadcasted_iota(jnp.int32, (samples, samples), 0)
    time = lax.broadcasted_iota(jnp.int32, (samples, samples), 1)
    piece = 256
    for number in range(widths_ref.shape[0]):
        width = widths_ref[number]
        begin = jnp.minimum(start, samples - width)
        inside = jnp.where((time >= begin) & (time < begin + width), 1.0, 0.0).astype(jnp.bfloat16)
        boxes[number, :, :samples] = inside
        boxes[number, :, samples:] = inside
    for part in range(total // piece):
        rows = series[part * piece:(part + 1) * piece]
        best = None
        for number in range(widths_ref.shape[0]):
            sums = lax.dot_general(
                boxes[number], rows, (((1,), (1,)), ((), ())), preferred_element_type=jnp.float32
            )
            norm = lax.rsqrt(jnp.full((1, piece), widths_ref[number] * CHANS, jnp.int32).astype(jnp.float32))
            peak = jnp.max(sums, axis=0, keepdims=True) * norm
            best = peak if best is None else jnp.maximum(best, peak)
        out_ref[0, :, part * piece:(part + 1) * piece] = best


def trial_peaks(rows, box_widths, place):
    beams, total, samples = rows.shape
    tiles = total // LANE_ROWS
    widths = box_widths.shape[0]
    return pl.pallas_call(
        trial_kernel,
        grid_spec=pltpu.PrefetchScalarGridSpec(
            num_scalar_prefetch=2,
            grid=(beams,),
            in_specs=[pl.BlockSpec((1, total, samples), lambda b, p, w: (b, 0, 0))],
            out_specs=pl.BlockSpec((1, 1, total), lambda b, p, w: (b, 0, 0)),
            scratch_shapes=[
                pltpu.VMEM((samples // 128, total, 128), jnp.float32),
                pltpu.VMEM((tiles, LANE_ROWS, samples), jnp.float32),
                pltpu.VMEM((tiles, LANE_ROWS, samples), jnp.float32),
                pltpu.VMEM((total, 2 * samples), jnp.bfloat16),
                pltpu.VMEM((widths, samples, 2 * samples), jnp.bfloat16),
            ],
        ),
        out_shape=jax.ShapeDtypeStruct((beams, 1, total), jnp.float32),
    )(place, box_widths, rows)[:, 0]


def shards(intensity, channel_mask, box_widths):
    group_count = lax.axis_size("beam")
    band_count = lax.axis_size("freq")
    beams_all, piece_width, samples = intensity.shape
    beam_dev = beams_all // group_count
    beam_place = lax.axis_index("beam").reshape(1)
    freq_place = lax.axis_index("freq").reshape(1)
    mask_rows = channel_mask.reshape(group_count, piece_width)
    rows = entry_rows(intensity, mask_rows, beam_place, band_count)
    bands = rows.shape[2]
    rows = rows.reshape(band_count * group_count, beam_dev * bands, samples)
    rows = lax.all_to_all(rows, ("freq", "beam"), split_axis=0, concat_axis=0, tiled=True)
    rows = rows.reshape(band_count * group_count, beam_dev, bands, samples)
    rows = jnp.swapaxes(rows, 0, 1).reshape(beam_dev, -1, samples)
    return trial_peaks(rows, box_widths, freq_place)


def solution(mesh):
    in_specs = (P(None, ("freq", "beam"), None), P("freq"), P())
    out_specs = P("beam", "freq")
    return jax.shard_map(shards, mesh=mesh, in_specs=in_specs, out_specs=out_specs, check_vma=False)
```

profile of v0, /device:TPU:0, one launch (start us, length us, event | category | flops | bytes accessed | tf_op | source)
XLA Modules:
  0.0 49.4 jit_solution(15958290899713073363)
XLA Ops:
  0.0 1.3 %reshape.14.mask_ref = s32[8,512]{1,0:T(8,128)} reshape(s32[4096]{0:T(1024)} %param.4) | data formatting | bytes 32768 | tf_op jit(solution)/shard_map/reshape | solution.py:227
  1.3 3.8 %shard_map.37 = bf16[4,8,32,256]{3,2,1,0:T(8,128)(2,1)} custom-call(s32[1]{0:T(128)} %bitcast.1.place_ref, bf16[8,512,256]{2,1,0:T(8,128)(2,1)} %x_ref.1, s32[8,512]{1,0:T(8,128)} %reshape.14.mask_ref), custom_call_target="tpu_custom_call" | custom-call | tf_op jit(solution)/shard_map/pallas_call | solution.py:82
  5.1 7.3 %all-to-all-start = ((bf16[32,32,256]{2,1,0:T(8,128)(2,1)}), bf16[32,32,256]{2,1,0:T(8,128)(2,1)S(1)}, u32[]{:S(2)}, u32[]{:S(2)}) async-start(bf16[32,32,256]{2,1,0:T(8,128)(2,1)} %bitcast.6), calls=%async_computation | async-start | bytes 1048576 | tf_op jit(solution)/shard_map/all_to_all | solution.py:231
  12.5 15.6 %all-to-all-done = bf16[32,32,256]{2,1,0:T(8,128)(2,1)S(1)} async-done(((bf16[32,32,256]{2,1,0:T(8,128)(2,1)}), bf16[32,32,256]{2,1,0:T(8,128)(2,1)S(1)}, u32[]{:S(2)}, u32[]{:S(2)}) %all-to-all-start) | async-done | bytes 524320 | tf_op jit(solution)/shard_map/all_to_all | solution.py:231
  28.1 0.0 copy-start
  28.1 0.8 %copy-done = bf16[32,32,256]{2,1,0:T(8,128)(2,1)} copy-done((bf16[32,32,256]{2,1,0:T(8,128)(2,1)}, bf16[32,32,256]{2,1,0:T(8,128)(2,1)S(1)}, u32[]{:S(2)}) %copy-start) | copy-done | bytes 524312
  28.9 20.5 %shard_map.38 = f32[1,1,1024]{2,1,0:T(1,128)} custom-call(s32[1]{0:T(128)} %bitcast.place_ref, s32[9]{0:T(128)} %widths_ref.1, bf16[1,1024,256]{2,1,0:T(8,128)(2,1)} %bitcast.5), custom_call_target="tpu_custom_call" | custom-call | tf_op jit(solution)/shard_map/pallas_call | solution.py:201
Async XLA Ops:
  5.1 23.0 %all-to-all-start = ((bf16[32,32,256]{2,1,0:T(8,128)(2,1)}), bf16[32,32,256]{2,1,0:T(8,128)(2,1)S(1)}, u32[]{:S(2)}, u32[]{:S(2)}) async-start(bf16[32,32,256]{2,1,0:T(8,128)(2,1)} %bitcast.6), calls=%async_computation | async-start | bytes 1048576 | tf_op jit(solution)/shard_map/all_to_all | solution.py:231
  28.1 0.8 %copy-start = (bf16[32,32,256]{2,1,0:T(8,128)(2,1)}, bf16[32,32,256]{2,1,0:T(8,128)(2,1)S(1)}, u32[]{:S(2)}) copy-start(bf16[32,32,256]{2,1,0:T(8,128)(2,1)S(1)} %all-to-all-done) | copy-start | bytes 1572868
where the time goes:
time: 49.7 us; the launch traced here: 49.4 us
  Pallas kernels  24.3 us (49%)
  waiting for transfers between devices  15.6 us (31%)
  starting transfers between devices  7.33 us (15%)
  local copies, waits for them, and re-layouts  2.11 us (4%)
    pallas_call x1, Pallas kernels, trial_peaks(): pl.pallas_call(trial_kernel, grid_spec=pltpu.PrefetchScalarGridSpec(num_s...  20.5 us
    all_to_all x1, waiting for transfers between devices, shards(): lax.all_to_all(rows, ('freq', 'beam'), split_axis=0, concat_axis=0, tiled...  15.6 us
    all_to_all x1, starting transfers between devices, shards(): lax.all_to_all(rows, ('freq', 'beam'), split_axis=0, concat_axis=0, tiled...  7.33 us
    pallas_call x1, Pallas kernels, entry_rows(): pl.pallas_call(functools.partial(entry_kernel, float(beams * samples)), g...  3.82 us
    reshape x1, local copies, waits for them, and re-layouts, shards(): mask_rows = channel_mask.reshape(group_count, piece_width)  1.32 us
  transfers between devices with their start and end apart: 1, of which 1 were waited for; matrix products, arithmetic and copies ran while one was open for 0% of the time, Pallas kernels for 0%

commit v1 on v0

v1 whole, which is shorter than its diff:
```python
import functools

import jax
import jax.numpy as jnp
from jax import lax
from jax.experimental import pallas as pl
from jax.experimental.pallas import tpu as pltpu
from jax.sharding import PartitionSpec as P

CHANS = 16384
NDM = 4096
LANE_ROWS = 8
LANES = 128
WIDEST = 64

epsilon = 1e-05


def reverse_bits(number, count):
    result = 0
    for _ in range(count):
        result = result << 1 | number & 1
        number >>= 1
    return result


def lane_index(shape):
    return lax.broadcasted_iota(jnp.int32, shape, len(shape) - 1)


def earlier(block, amount):
    if amount == 0:
        return block
    samples = block.shape[-1]
    return jnp.where(lane_index(block.shape) < samples - amount, pltpu.roll(block, samples - amount, 1), 0.0)


def entry_kernel(row_total, place_ref, x_ref, mask_ref, out_ref):
    rows, beams, bands, samples = out_ref.shape
    width = x_ref.shape[1]
    group = width // (bands * rows)
    total = jnp.zeros((width, samples), jnp.float32)
    squares = jnp.zeros((width, samples), jnp.float32)
    for beam in range(beams):
        wide = x_ref[beam].astype(jnp.float32)
        total = total + wide
        squares = squares + wide * wide
    channel_mean = jnp.sum(total, axis=1, keepdims=True) / row_total
    channel_var = jnp.sum(squares, axis=1, keepdims=True) / row_total - channel_mean * channel_mean
    channel_scale = lax.rsqrt(channel_var + epsilon)
    out_row = lax.broadcasted_iota(jnp.int32, (rows * bands, width), 0)
    channel = lax.broadcasted_iota(jnp.int32, (rows * bands, width), 1)
    wanted = (out_row % bands) * rows + out_row // bands
    clean = mask_ref[pl.ds(place_ref[0], 1), :].astype(jnp.float32)
    chosen = jnp.where(channel // group == wanted, clean, 0.0).astype(jnp.bfloat16)
    for beam in range(beams):
        wide = x_ref[beam].astype(jnp.float32)
        normed = ((wide - channel_mean) * channel_scale).astype(jnp.bfloat16)
        sums = jnp.dot(chosen, normed, preferred_element_type=jnp.float32)
        tree = [[sums[i * bands:(i + 1) * bands]] for i in range(rows)]
        while len(tree) > 1:
            merged = []
            for low, high in zip(tree[0::2], tree[1::2]):
                merged.append(
                    [low[m // 2] + earlier(high[m // 2], (m + 1) // 2) for m in range(2 * len(low))]
                )
            tree = merged
        for number, row in enumerate(tree[0]):
            out_ref[number, beam] = row.astype(jnp.bfloat16)


def entry_rows(intensity, mask_rows, place, rows):
    beams, width, samples = intensity.shape
    bands = width * NDM // (CHANS * rows)
    chunks = 2 if bands % 32 == 0 else 1
    return pl.pallas_call(
        functools.partial(entry_kernel, float(beams * samples)),
        grid_spec=pltpu.PrefetchScalarGridSpec(
            num_scalar_prefetch=1,
            grid=(chunks,),
            in_specs=[
                pl.BlockSpec((beams, width // chunks, samples), lambda c, p: (0, c, 0)),
                pl.BlockSpec((mask_rows.shape[0], width // chunks), lambda c, p: (0, c)),
            ],
            out_specs=pl.BlockSpec((rows, beams, bands // chunks, samples), lambda c, p: (0, 0, c, 0)),
        ),
        out_shape=jax.ShapeDtypeStruct((rows, beams, bands, samples), jnp.bfloat16),
    )(place, intensity, mask_rows)


def advanced(pieces, amount):
    lanes = pieces[0].shape[-1]
    position = lane_index(pieces[0].shape)
    turn = (lanes - amount) & (lanes - 1)
    turned = [pltpu.roll(piece, turn, 1) for piece in pieces]
    return joined(turned, lambda limit: position < limit - amount)


def advanced_rows(pieces, amounts):
    lanes = pieces[0].shape[-1]
    position = lane_index(pieces[0].shape) + amounts
    picks = position & (lanes - 1)
    turned = [jnp.take_along_axis(piece, picks, axis=1, mode="promise_in_bounds") for piece in pieces]
    return joined(turned, lambda limit: position < limit)


def joined(turned, below):
    lanes = turned[0].shape[-1]
    near = [below((k + 1) * lanes) for k in range(len(turned))]
    result = []
    for number in range(len(turned)):
        value = jnp.zeros_like(turned[0])
        for ahead in reversed(range(len(turned) - number)):
            value = jnp.where(near[ahead], turned[number + ahead], value)
        result.append(value)
    return result


def trial_kernel(place_ref, widths_ref, x_ref, out_ref, first, even, odd, series, prefix):
    total, samples = x_ref.shape[1:]
    tiles = total // LANE_ROWS
    tile_bits = tiles.bit_length() - 1
    lanes = prefix.shape[2]
    parts = samples // lanes
    pitch = first.shape[1] // LANE_ROWS
    block = place_ref[0]
    for high in range(LANE_ROWS):
        spot = reverse_bits(high, LANE_ROWS.bit_length() - 1)
        for part in range(parts):
            first[part, spot * pitch:spot * pitch + tiles] = x_ref[
                0, high * tiles:(high + 1) * tiles, part * lanes:(part + 1) * lanes
            ].astype(jnp.float32)
    for tile in range(tiles):
        for part in range(parts):
            even[reverse_bits(tile, tile_bits), :, part * lanes:(part + 1) * lanes] = first[
                part, pl.ds(tile, LANE_ROWS, stride=pitch)
            ]

    source, target = even, odd
    count = 1
    while count < tiles:
        half = tiles // count // 2

        def merge(j, source=source, target=target, count=count, half=half):
            flat = (half * LANE_ROWS, lanes)
            cut = [slice(part * lanes, (part + 1) * lanes) for part in range(parts)]
            low = [source[pl.ds(j * 2 * half, half), :, c].reshape(flat) for c in cut]
            high = [source[pl.ds(j * 2 * half + half, half), :, c].reshape(flat) for c in cut]
            for side in range(2):
                moved = advanced(high, block * count + j + side)
                for c, base, extra in zip(cut, low, moved):
                    target[pl.ds((2 * j + side) * half, half), :, c] = (base + extra).reshape(
                        half, LANE_ROWS, lanes
                    )

        if count <= 16:
            for j in range(count):
                merge(j)
        else:
            def step(i, carry, merge=merge):
                for k in range(32):
                    merge(i * 32 + k)
                return carry
            lax.fori_loop(0, count // 32, step, 0)
        source, target = target, source
        count = count * 2

    spot = lax.broadcasted_iota(jnp.int32, (LANE_ROWS, lanes), 0)
    bits = [spot >> 2 & 1, spot >> 1 & 1, spot & 1]
    clear = [bit == 0 for bit in bits]

    def final_rows(j):
        pieces = [source[j, :, part * lanes:(part + 1) * lanes] for part in range(parts)]
        row = spot * 0 + (block * tiles + j)
        for level, reach in enumerate((4, 2, 1)):
            low, high = [], []
            for piece in pieces:
                down = pltpu.roll(piece, reach, 0)
                up = down if 2 * reach == LANE_ROWS else pltpu.roll(piece, LANE_ROWS - reach, 0)
                low.append(jnp.where(clear[level], piece, down))
                high.append(jnp.where(clear[level], up, piece))
            moved = advanced_rows(high, row + bits[level])
            pieces = [base + extra for base, extra in zip(low, moved)]
            row = 2 * row + bits[level]
        return jnp.concatenate(pieces, axis=1)

    def finish(i, carry):
        for k in range(16):
            pair = i * 16 + k
            rows = jnp.concatenate([final_rows(2 * pair), final_rows(2 * pair + 1)], axis=0)
            coarse = rows.astype(jnp.bfloat16)
            place = pl.ds(pl.multiple_of(pair * 16, 16), 16)
            series[place, :samples] = coarse
            series[place, samples:] = (rows - coarse.astype(jnp.float32)).astype(jnp.bfloat16)
        return carry

    lax.fori_loop(0, tiles // 32, finish, 0)

    until = lax.broadcasted_iota(jnp.int32, (samples, 2 * samples), 0)
    time = lax.broadcasted_iota(jnp.int32, (samples, 2 * samples), 1) & (samples - 1)
    ladder = jnp.where(time <= until, 1.0, 0.0).astype(jnp.bfloat16)
    margin = prefix.shape[1] - samples - LANE_ROWS
    piece = 2 * lanes
    for part in range(total // piece):
        sums = lax.dot_general(
            ladder, series[part * piece:(part + 1) * piece], (((1,), (1,)), ((), ())),
            preferred_element_type=jnp.float32,
        )
        for side in range(2):
            column = 2 * part + side
            prefix[column, :LANE_ROWS] = jnp.zeros((LANE_ROWS, lanes), jnp.float32)
            prefix[column, LANE_ROWS:LANE_ROWS + samples] = sums[:, side * lanes:(side + 1) * lanes]
            prefix[column, LANE_ROWS + samples:] = jnp.full((margin, lanes), -jnp.inf, jnp.float32)
    for column in range(total // lanes):
        best = None
        for number in range(widths_ref.shape[0]):
            width = widths_ref[number]
            sums = (
                prefix[column, pl.ds(LANE_ROWS - 1 + width, samples)]
                - prefix[column, LANE_ROWS - 1:LANE_ROWS - 1 + samples]
            )
            norm = lax.rsqrt(jnp.full((1, lanes), width * CHANS, jnp.int32).astype(jnp.float32))
            peak = jnp.max(sums, axis=0, keepdims=True) * norm
            best = peak if best is None else jnp.maximum(best, peak)
        out_ref[0, :, column * lanes:(column + 1) * lanes] = best


def trial_peaks(rows, box_widths, place):
    beams, total, samples = rows.shape
    tiles = total // LANE_ROWS
    return pl.pallas_call(
        trial_kernel,
        grid_spec=pltpu.PrefetchScalarGridSpec(
            num_scalar_prefetch=2,
            grid=(beams,),
            in_specs=[pl.BlockSpec((1, total, samples), lambda b, p, w: (b, 0, 0))],
            out_specs=pl.BlockSpec((1, 1, total), lambda b, p, w: (b, 0, 0)),
            scratch_shapes=[
                pltpu.VMEM((samples // LANES, total + LANE_ROWS * LANE_ROWS, LANES), jnp.float32),
                pltpu.VMEM((tiles, LANE_ROWS, samples), jnp.float32),
                pltpu.VMEM((tiles, LANE_ROWS, samples), jnp.float32),
                pltpu.VMEM((total, 2 * samples), jnp.bfloat16),
                pltpu.VMEM((total // LANES, LANE_ROWS + samples + WIDEST, LANES), jnp.float32),
            ],
        ),
        out_shape=jax.ShapeDtypeStruct((beams, 1, total), jnp.float32),
    )(place, box_widths, rows)[:, 0]


def shards(intensity, channel_mask, box_widths):
    group_count = lax.axis_size("beam")
    band_count = lax.axis_size("freq")
    beams_all, piece_width, samples = intensity.shape
    beam_dev = beams_all // group_count
    beam_place = lax.axis_index("beam").reshape(1)
    freq_place = lax.axis_index("freq").reshape(1)
    mask_rows = channel_mask.reshape(group_count, piece_width)
    rows = entry_rows(intensity, mask_rows, beam_place, band_count)
    bands = rows.shape[2]
    rows = rows.reshape(band_count * group_count, beam_dev * bands, samples)
    rows = lax.all_to_all(rows, ("freq", "beam"), split_axis=0, concat_axis=0, tiled=True)
    rows = rows.reshape(band_count * group_count, beam_dev, bands, samples)
    rows = jnp.swapaxes(rows, 0, 1).reshape(beam_dev, -1, samples)
    return trial_peaks(rows, box_widths, freq_place)


def solution(mesh):
    in_specs = (P(None, ("freq", "beam"), None), P("freq"), P())
    out_specs = P("beam", "freq")
    return jax.shard_map(shards, mesh=mesh, in_specs=in_specs, out_specs=out_specs, check_vma=False)
```

time: 49.7 us -> 41.4 us (0.83)
  Pallas kernels: 24.3 us -> 16.1 us
    pallas_call x1, Pallas kernels: 20.5 us -> 12.2 us  [trial_peaks(): pl.pallas_call(trial_kernel, grid_spec=pltpu.PrefetchScalarGridSpec(num_s...]
where the time goes in v1:
time: 41.4 us; the launch traced here: 41.1 us
  Pallas kernels  16.1 us (39%)
  waiting for transfers between devices  15.6 us (38%)
  starting transfers between devices  7.33 us (18%)
  local copies, waits for them, and re-layouts  2.11 us (5%)
    all_to_all x1, waiting for transfers between devices, shards(): lax.all_to_all(rows, ('freq', 'beam'), split_axis=0, concat_axis=0, tiled...  15.6 us
    pallas_call x1, Pallas kernels, trial_peaks(): pl.pallas_call(trial_kernel, grid_spec=pltpu.PrefetchScalarGridSpec(num_s...  12.2 us
    all_to_all x1, starting transfers between devices, shards(): lax.all_to_all(rows, ('freq', 'beam'), split_axis=0, concat_axis=0, tiled...  7.33 us
    pallas_call x1, Pallas kernels, entry_rows(): pl.pallas_call(functools.partial(entry_kernel, float(beams * samples)), g...  3.82 us
    reshape x1, local copies, waits for them, and re-layouts, shards(): mask_rows = channel_mask.reshape(group_count, piece_width)  1.32 us
  transfers between devices with their start and end apart: 1, of which 1 were waited for; matrix products, arithmetic and copies ran while one was open for 0% of the time, Pallas kernels for 0%

profile of v1, /device:TPU:0, one launch (start us, length us, event | category | flops | bytes accessed | tf_op | source)
XLA Modules:
  0.0 41.1 jit_solution(5164906308150148959)
XLA Ops:
  0.0 1.3 %reshape.14.mask_ref = s32[8,512]{1,0:T(8,128)} reshape(s32[4096]{0:T(1024)} %param.4) | data formatting | bytes 32768 | tf_op jit(solution)/shard_map/reshape | solution.py:257
  1.3 3.8 %shard_map.37 = bf16[4,8,32,256]{3,2,1,0:T(8,128)(2,1)} custom-call(s32[1]{0:T(128)} %bitcast.1.place_ref, bf16[8,512,256]{2,1,0:T(8,128)(2,1)} %x_ref.1, s32[8,512]{1,0:T(8,128)} %reshape.14.mask_ref), custom_call_target="tpu_custom_call" | custom-call | tf_op jit(solution)/shard_map/pallas_call | solution.py:76
  5.1 7.3 %all-to-all-start = ((bf16[32,32,256]{2,1,0:T(8,128)(2,1)}), bf16[32,32,256]{2,1,0:T(8,128)(2,1)S(1)}, u32[]{:S(2)}, u32[]{:S(2)}) async-start(bf16[32,32,256]{2,1,0:T(8,128)(2,1)} %bitcast.6), calls=%async_computation | async-start | bytes 1048576 | tf_op jit(solution)/shard_map/all_to_all | solution.py:261
  12.5 15.6 %all-to-all-done = bf16[32,32,256]{2,1,0:T(8,128)(2,1)S(1)} async-done(((bf16[32,32,256]{2,1,0:T(8,128)(2,1)}), bf16[32,32,256]{2,1,0:T(8,128)(2,1)S(1)}, u32[]{:S(2)}, u32[]{:S(2)}) %all-to-all-start) | async-done | bytes 524320 | tf_op jit(solution)/shard_map/all_to_all | solution.py:261
  28.1 0.0 copy-start
  28.1 0.8 %copy-done = bf16[32,32,256]{2,1,0:T(8,128)(2,1)} copy-done((bf16[32,32,256]{2,1,0:T(8,128)(2,1)}, bf16[32,32,256]{2,1,0:T(8,128)(2,1)S(1)}, u32[]{:S(2)}) %copy-start) | copy-done | bytes 524312
  28.9 12.2 %shard_map.38 = f32[1,1,1024]{2,1,0:T(1,128)} custom-call(s32[1]{0:T(128)} %bitcast.place_ref, s32[9]{0:T(128)} %widths_ref.1, bf16[1,1024,256]{2,1,0:T(8,128)(2,1)} %bitcast.5), custom_call_target="tpu_custom_call" | custom-call | tf_op jit(solution)/shard_map/pallas_call | solution.py:231
Async XLA Ops:
  5.1 23.0 %all-to-all-start = ((bf16[32,32,256]{2,1,0:T(8,128)(2,1)}), bf16[32,32,256]{2,1,0:T(8,128)(2,1)S(1)}, u32[]{:S(2)}, u32[]{:S(2)}) async-start(bf16[32,32,256]{2,1,0:T(8,128)(2,1)} %bitcast.6), calls=%async_computation | async-start | bytes 1048576 | tf_op jit(solution)/shard_map/all_to_all | solution.py:261
  28.1 0.8 %copy-start = (bf16[32,32,256]{2,1,0:T(8,128)(2,1)}, bf16[32,32,256]{2,1,0:T(8,128)(2,1)S(1)}, u32[]{:S(2)}) copy-start(bf16[32,32,256]{2,1,0:T(8,128)(2,1)S(1)} %all-to-all-done) | copy-start | bytes 1572868

commit v2 on v1

--- a/solution.py
+++ b/solution.py
@@ -1,5 +1,3 @@
-import functools
-
 import jax
 import jax.numpy as jnp
 from jax import lax
@@ -35,10 +33,43 @@
     return jnp.where(lane_index(block.shape) < samples - amount, pltpu.roll(block, samples - amount, 1), 0.0)
 
 
-def entry_kernel(row_total, place_ref, x_ref, mask_ref, out_ref):
-    rows, beams, bands, samples = out_ref.shape
+def folds(trial_dev, samples):
+    return trial_dev >= 4 * samples
+
+
+def channel_limits(trial_dev, blocks, samples):
+    limits = []
+    for block in range(blocks):
+        limit, rows = CHANS, NDM
+        while (block * trial_dev * rows // NDM + 1) // 2 >= samples:
+            limit, rows = limit // 2, rows // 2
+        limits.append(limit)
+    return limits
+
+
+def entry_kernel(x_ref, mask_ref, out_ref, send, send_sem, recv_sem, own_sem):
+    blocks, beams, bands, samples = send.shape
+    groups = lax.axis_size("beam")
+    beam_dev = beams // groups
     width = x_ref.shape[1]
-    group = width // (bands * rows)
+    group = width // (bands * blocks)
+    trial_dev = NDM // blocks
+    row_total = float(beams * samples)
+    fold = folds(trial_dev, samples)
+    limits = channel_limits(trial_dev, blocks, samples)
+    my_block = lax.axis_index("freq")
+    my_group = lax.axis_index("beam")
+    my_place = my_block * groups + my_group
+    devices = blocks * groups
+
+    barrier = pltpu.get_barrier_semaphore()
+    for step in range(1, devices):
+        peer = (my_place + step) % devices
+        pl.semaphore_signal(
+            barrier, inc=1, device_id={"freq": peer // groups, "beam": peer % groups},
+            device_id_type=pl.DeviceIdType.MESH,
+        )
+
     total = jnp.zeros((width, samples), jnp.float32)
     squares = jnp.zeros((width, samples), jnp.float32)
     for beam in range(beams):
@@ -48,16 +79,54 @@
     channel_mean = jnp.sum(total, axis=1, keepdims=True) / row_total
     channel_var = jnp.sum(squares, axis=1, keepdims=True) / row_total - channel_mean * channel_mean
     channel_scale = lax.rsqrt(channel_var + epsilon)
-    out_row = lax.broadcasted_iota(jnp.int32, (rows * bands, width), 0)
-    channel = lax.broadcasted_iota(jnp.int32, (rows * bands, width), 1)
-    wanted = (out_row % bands) * rows + out_row // bands
-    clean = mask_ref[pl.ds(place_ref[0], 1), :].astype(jnp.float32)
+    out_row = lax.broadcasted_iota(jnp.int32, (blocks * bands, width), 0)
+    channel = lax.broadcasted_iota(jnp.int32, (blocks * bands, width), 1)
+    band = out_row % bands
+    if fold:
+        half = bands // 2
+        band = (band % half) * 2 + band // half
+    wanted = band * blocks + out_row // bands
+    clean = mask_ref[:, pl.ds(pl.multiple_of(my_group * width, width), width)].astype(jnp.float32)
     chosen = jnp.where(channel // group == wanted, clean, 0.0).astype(jnp.bfloat16)
-    for beam in range(beams):
+    upper = my_block * 2 >= blocks
+
+    def message(block, slot, beam, rows):
+        return pltpu.make_async_remote_copy(
+            src_ref=send.at[block, slot, pl.ds(0, rows)],
+            dst_ref=out_ref.at[beam % beam_dev, my_place, pl.ds(0, rows)],
+            send_sem=send_sem.at[block, slot],
+            recv_sem=recv_sem.at[beam % beam_dev, my_place],
+            device_id={"freq": block, "beam": beam // beam_dev},
+            device_id_type=pl.DeviceIdType.MESH,
+        )
+
+    def own_copy(slot, part):
+        return pltpu.make_async_copy(
+            send.at[my_block, slot], out_ref.at[part, my_place], own_sem.at[part]
+        )
+
+    def every_message(action, slot):
+        beam = (my_group * beam_dev + slot) % beams
+        for block in range(blocks):
+            goes = my_place * width < limits[block]
+            if slot < beam_dev:
+                goes = goes & (my_block != block)
+            if fold:
+                @pl.when(goes & upper)
+                def _(block=block):
+                    action(message(block, slot, beam, bands // 2))
+                goes = goes & jnp.logical_not(upper)
+
+            @pl.when(goes)
+            def _(block=block):
+                action(message(block, slot, beam, bands))
+
+    for slot in range(beams):
+        beam = (my_group * beam_dev + slot) % beams
         wide = x_ref[beam].astype(jnp.float32)
         normed = ((wide - channel_mean) * channel_scale).astype(jnp.bfloat16)
         sums = jnp.dot(chosen, normed, preferred_element_type=jnp.float32)
-        tree = [[sums[i * bands:(i + 1) * bands]] for i in range(rows)]
+        tree = [[sums[i * bands:(i + 1) * bands]] for i in range(blocks)]
         while len(tree) > 1:
             merged = []
             for low, high in zip(tree[0::2], tree[1::2]):
@@ -66,26 +135,53 @@
                 )
             tree = merged
         for number, row in enumerate(tree[0]):
-            out_ref[number, beam] = row.astype(jnp.bfloat16)
-
-
-def entry_rows(intensity, mask_rows, place, rows):
+            if fold:
+                both = row[:half] + row[half:]
+                row = jnp.concatenate([jnp.where(upper, both, row[:half]), row[half:]], axis=0)
+            send[number, slot] = row.astype(jnp.bfloat16)
+        if slot == 0:
+            pl.semaphore_wait(barrier, devices - 1)
+        every_message(lambda copy: copy.start(), slot)
+        if slot < beam_dev:
+            own_copy(slot, slot).start()
+
+    for slot in range(beam_dev):
+        own_copy(slot, slot).wait()
+    limit = sum(jnp.where(my_block == block, limits[block], 0) for block in range(blocks))
+    for place in range(devices):
+        for part in range(beam_dev):
+            rows = bands // 2 if fold and 2 * place >= devices else bands
+            target = out_ref.at[part, place, pl.ds(0, rows)]
+            @pl.when((place * width < limit) & (place != my_place))
+            def _(target=target, place=place, part=part):
+                pltpu.make_async_remote_copy(
+                    src_ref=target, dst_ref=target, send_sem=send_sem.at[0, 0],
+                    recv_sem=recv_sem.at[part, place],
+                    device_id={"freq": my_block, "beam": my_group},
+                    device_id_type=pl.DeviceIdType.MESH,
+                ).wait_recv()
+    for slot in range(beams):
+        every_message(lambda copy: copy.wait_send(), slot)
+
+
+def entry_rows(intensity, channel_mask):
     beams, width, samples = intensity.shape
-    bands = width * NDM // (CHANS * rows)
-    chunks = 2 if bands % 32 == 0 else 1
+    blocks, groups = lax.axis_size("freq"), lax.axis_size("beam")
+    bands = width * NDM // (CHANS * blocks)
+    beam_dev, devices = beams // groups, blocks * groups
     return pl.pallas_call(
-        functools.partial(entry_kernel, float(beams * samples)),
-        grid_spec=pltpu.PrefetchScalarGridSpec(
-            num_scalar_prefetch=1,
-            grid=(chunks,),
-            in_specs=[
-                pl.BlockSpec((beams, width // chunks, samples), lambda c, p: (0, c, 0)),
-                pl.BlockSpec((mask_rows.shape[0], width // chunks), lambda c, p: (0, c)),
-            ],
-            out_specs=pl.BlockSpec((rows, beams, bands // chunks, samples), lambda c, p: (0, 0, c, 0)),
-        ),
-        out_shape=jax.ShapeDtypeStruct((rows, beams, bands, samples), jnp.bfloat16),
-    )(place, intensity, mask_rows)
+        entry_kernel,
+        in_specs=[pl.BlockSpec(memory_space=pltpu.VMEM)] * 2,
+        out_specs=pl.BlockSpec(memory_space=pl.ANY),
+        scratch_shapes=[
+            pltpu.VMEM((blocks, beams, bands, samples), jnp.bfloat16),
+            pltpu.SemaphoreType.DMA((blocks, beams)),
+            pltpu.SemaphoreType.DMA((beam_dev, devices)),
+            pltpu.SemaphoreType.DMA((beam_dev,)),
+        ],
+        out_shape=jax.ShapeDtypeStruct((beam_dev, devices, bands, samples), jnp.bfloat16),
+        compiler_params=pltpu.CompilerParams(collective_id=0, has_side_effects=True),
+    )(intensity, channel_mask.reshape(1, -1))
 
 
 def advanced(pieces, amount):
@@ -117,23 +213,35 @@
 
 
 def trial_kernel(place_ref, widths_ref, x_ref, out_ref, first, even, odd, series, prefix):
-    total, samples = x_ref.shape[1:]
+    total, samples = out_ref.shape[2], x_ref.shape[3]
     tiles = total // LANE_ROWS
     tile_bits = tiles.bit_length() - 1
     lanes = prefix.shape[2]
     parts = samples // lanes
     pitch = first.shape[1] // LANE_ROWS
     block = place_ref[0]
-    for high in range(LANE_ROWS):
-        spot = reverse_bits(high, LANE_ROWS.bit_length() - 1)
+    bands = x_ref.shape[2]
+    fold = folds(total, samples)
+    half_bands = bands // 2
+    sources = x_ref.shape[1]
+    for number in range(sources):
+        high, start = divmod(number * bands, tiles)
+        start += reverse_bits(high, LANE_ROWS.bit_length() - 1) * pitch
         for part in range(parts):
-            first[part, spot * pitch:spot * pitch + tiles] = x_ref[
-                0, high * tiles:(high + 1) * tiles, part * lanes:(part + 1) * lanes
-            ].astype(jnp.float32)
+            cut = slice(part * lanes, (part + 1) * lanes)
+            if fold and 2 * number >= sources:
+                first[part, start:start + half_bands] = x_ref[0, number, :half_bands, cut].astype(jnp.float32)
+                first[part, start + half_bands:start + bands] = jnp.zeros((half_bands, lanes), jnp.float32)
+            else:
+                first[part, start:start + bands] = x_ref[0, number, :, cut].astype(jnp.float32)
     for tile in range(tiles):
+        spot = tile
+        if fold:
+            band = tile % bands
+            spot = tile - band + (band % 2) * half_bands + band // 2
         for part in range(parts):
             even[reverse_bits(tile, tile_bits), :, part * lanes:(part + 1) * lanes] = first[
-                part, pl.ds(tile, LANE_ROWS, stride=pitch)
+                part, pl.ds(spot, LANE_ROWS, stride=pitch)
             ]
 
     source, target = even, odd
@@ -226,14 +334,15 @@
 
 
 def trial_peaks(rows, box_widths, place):
-    beams, total, samples = rows.shape
+    beams, devices, bands, samples = rows.shape
+    total = devices * bands
     tiles = total // LANE_ROWS
     return pl.pallas_call(
         trial_kernel,
         grid_spec=pltpu.PrefetchScalarGridSpec(
             num_scalar_prefetch=2,
             grid=(beams,),
-            in_specs=[pl.BlockSpec((1, total, samples), lambda b, p, w: (b, 0, 0))],
+            in_specs=[pl.BlockSpec((1, devices, bands, samples), lambda b, p, w: (b, 0, 0, 0))],
             out_specs=pl.BlockSpec((1, 1, total), lambda b, p, w: (b, 0, 0)),
             scratch_shapes=[
                 pltpu.VMEM((samples // LANES, total + LANE_ROWS * LANE_ROWS, LANES), jnp.float32),
@@ -248,20 +357,8 @@
 
 
 def shards(intensity, channel_mask, box_widths):
-    group_count = lax.axis_size("beam")
-    band_count = lax.axis_size("freq")
-    beams_all, piece_width, samples = intensity.shape
-    beam_dev = beams_all // group_count
-    beam_place = lax.axis_index("beam").reshape(1)
-    freq_place = lax.axis_index("freq").reshape(1)
-    mask_rows = channel_mask.reshape(group_count, piece_width)
-    rows = entry_rows(intensity, mask_rows, beam_place, band_count)
-    bands = rows.shape[2]
-    rows = rows.reshape(band_count * group_count, beam_dev * bands, samples)
-    rows = lax.all_to_all(rows, ("freq", "beam"), split_axis=0, concat_axis=0, tiled=True)
-    rows = rows.reshape(band_count * group_count, beam_dev, bands, samples)
-    rows = jnp.swapaxes(rows, 0, 1).reshape(beam_dev, -1, samples)
-    return trial_peaks(rows, box_widths, freq_place)
+    rows = entry_rows(intensity, channel_mask)
+    return trial_peaks(rows, box_widths, lax.axis_index("freq").reshape(1))
 
 
 def solution(mesh):

time: 41.4 us -> 30.5 us (0.74)
  waiting for transfers between devices: 15.6 us -> 0 us
  Pallas kernels: 16.1 us -> 30.3 us
  starting transfers between devices: 7.33 us -> 0 us
  local copies, waits for them, and re-layouts: 2.11 us -> 0 us
    all_to_all x1 -> x0, waiting for transfers between devices: 15.6 us -> none  [shards(): lax.all_to_all(rows, ('freq', 'beam'), split_axis=0, concat_axis=0, tiled...]
    pallas_call x1, Pallas kernels: 3.82 us -> 18.1 us  [entry_rows(): pl.pallas_call(entry_kernel, in_specs=[pl.BlockSpec(memory_space=pltpu.VM...]
    all_to_all x1 -> x0, starting transfers between devices: 7.33 us -> none  [shards(): lax.all_to_all(rows, ('freq', 'beam'), split_axis=0, concat_axis=0, tiled...]
    reshape x1 -> x0, local copies, waits for them, and re-layouts: 1.32 us -> none  [shards(): mask_rows = channel_mask.reshape(group_count, piece_width)]
    unnamed x2 -> x0, local copies, waits for them, and re-layouts: 0.79 us -> none
  transfers between devices with their start and end apart: 1 -> 0, of which waited for: 1 -> 0; matrix products, arithmetic and copies ran while one was open for 0% -> 0% of each run, Pallas kernels for 0% -> 0%
where the time goes in v2:
time: 30.5 us; the launch traced here: 30.3 us
  Pallas kernels  30.3 us (99%)
    pallas_call x1, Pallas kernels, entry_rows(): pl.pallas_call(entry_kernel, in_specs=[pl.BlockSpec(memory_space=pltpu.VM...  18.1 us
    pallas_call x1, Pallas kernels, trial_peaks(): pl.pallas_call(trial_kernel, grid_spec=pltpu.PrefetchScalarGridSpec(num_s...  12.2 us

profile of v2, /device:TPU:0, one launch (start us, length us, event | category | flops | bytes accessed | tf_op | source)
XLA Modules:
  0.0 30.3 jit_solution(5912039235722043674)
XLA Ops:
  0.0 18.1 %shard_map.37.x_ref = bf16[1,32,32,256]{3,2,1,0:T(8,128)(2,1)} custom-call(bf16[8,512,256]{2,1,0:T(8,128)(2,1)} %x_ref.1, s32[1,4096]{1,0:T(1,128)} %bitcast.3), custom_call_target="tpu_custom_call" | custom-call | tf_op jit(solution)/shard_map/pallas_call | solution.py:172
  18.1 12.2 %shard_map.38 = f32[1,1,1024]{2,1,0:T(1,128)} custom-call(s32[1]{0:T(128)} %bitcast.place_ref, s32[9]{0:T(128)} %widths_ref.1, bf16[1,32,32,256]{3,2,1,0:T(8,128)(2,1)} %shard_map.37.x_ref), custom_call_target="tpu_custom_call" | custom-call | tf_op jit(solution)/shard_map/pallas_call | solution.py:340

commit v3 on v2

--- a/solution.py
+++ b/solution.py
@@ -47,7 +47,7 @@
     return limits
 
 
-def entry_kernel(x_ref, mask_ref, out_ref, send, send_sem, recv_sem, own_sem):
+def entry_kernel(x_hbm, mask_ref, out_ref, x_ref, in_sem, send, send_sem, recv_sem, own_sem):
     blocks, beams, bands, samples = send.shape
     groups = lax.axis_size("beam")
     beam_dev = beams // groups
@@ -70,15 +70,31 @@
             device_id_type=pl.DeviceIdType.MESH,
         )
 
-    total = jnp.zeros((width, samples), jnp.float32)
-    squares = jnp.zeros((width, samples), jnp.float32)
-    for beam in range(beams):
-        wide = x_ref[beam].astype(jnp.float32)
-        total = total + wide
-        squares = squares + wide * wide
-    channel_mean = jnp.sum(total, axis=1, keepdims=True) / row_total
-    channel_var = jnp.sum(squares, axis=1, keepdims=True) / row_total - channel_mean * channel_mean
-    channel_scale = lax.rsqrt(channel_var + epsilon)
+    chunks = in_sem.shape[0]
+    span = width // chunks
+    loads = [
+        pltpu.make_async_copy(
+            x_hbm.at[:, pl.ds(c * span, span)], x_ref.at[:, pl.ds(c * span, span)], in_sem.at[c]
+        )
+        for c in range(chunks)
+    ]
+    for load in loads:
+        load.start()
+    means, scales = [], []
+    for c in range(chunks):
+        loads[c].wait()
+        total = jnp.zeros((span, samples), jnp.float32)
+        squares = jnp.zeros((span, samples), jnp.float32)
+        for beam in range(beams):
+            wide = x_ref[beam, c * span:(c + 1) * span].astype(jnp.float32)
+            total = total + wide
+            squares = squares + wide * wide
+        mean = jnp.sum(total, axis=1, keepdims=True) / row_total
+        var = jnp.sum(squares, axis=1, keepdims=True) / row_total - mean * mean
+        means.append(mean)
+        scales.append(lax.rsqrt(var + epsilon))
+    channel_mean = jnp.concatenate(means, axis=0)
+    channel_scale = jnp.concatenate(scales, axis=0)
     out_row = lax.broadcasted_iota(jnp.int32, (blocks * bands, width), 0)
     channel = lax.broadcasted_iota(jnp.int32, (blocks * bands, width), 1)
     band = out_row % bands
@@ -171,9 +187,11 @@
     beam_dev, devices = beams // groups, blocks * groups
     return pl.pallas_call(
         entry_kernel,
-        in_specs=[pl.BlockSpec(memory_space=pltpu.VMEM)] * 2,
+        in_specs=[pl.BlockSpec(memory_space=pl.ANY), pl.BlockSpec(memory_space=pltpu.VMEM)],
         out_specs=pl.BlockSpec(memory_space=pl.ANY),
         scratch_shapes=[
+            pltpu.VMEM((beams, width, samples), jnp.bfloat16),
+            pltpu.SemaphoreType.DMA((4,)),
             pltpu.VMEM((blocks, beams, bands, samples), jnp.bfloat16),
             pltpu.SemaphoreType.DMA((blocks, beams)),
             pltpu.SemaphoreType.DMA((beam_dev, devices)),

time: 30.5 us -> 29.7 us (0.974)
  Pallas kernels: 30.3 us -> 29.4 us
    pallas_call x1, Pallas kernels: 18.1 us -> 17.2 us  [entry_rows(): pl.pallas_call(entry_kernel, in_specs=[pl.BlockSpec(memory_space=pl.ANY),...]
where the time goes in v3:
time: 29.7 us; the launch traced here: 29.4 us
  Pallas kernels  29.4 us (99%)
    pallas_call x1, Pallas kernels, entry_rows(): pl.pallas_call(entry_kernel, in_specs=[pl.BlockSpec(memory_space=pl.ANY),...  17.2 us
    pallas_call x1, Pallas kernels, trial_peaks(): pl.pallas_call(trial_kernel, grid_spec=pltpu.PrefetchScalarGridSpec(num_s...  12.2 us

profile of v3, /device:TPU:0, one launch (start us, length us, event | category | flops | bytes accessed | tf_op | source)
XLA Modules:
  0.0 29.4 jit_solution(597220869878629304)
XLA Ops:
  0.0 17.2 %shard_map.37.x_ref = bf16[1,32,32,256]{3,2,1,0:T(8,128)(2,1)} custom-call(bf16[8,512,256]{2,1,0:T(8,128)(2,1)} %x_hbm.1, s32[1,4096]{1,0:T(1,128)} %bitcast.3), custom_call_target="tpu_custom_call" | custom-call | tf_op jit(solution)/shard_map/pallas_call | solution.py:188
  17.2 12.2 %shard_map.38 = f32[1,1,1024]{2,1,0:T(1,128)} custom-call(s32[1]{0:T(128)} %bitcast.place_ref, s32[9]{0:T(128)} %widths_ref.1, bf16[1,32,32,256]{3,2,1,0:T(8,128)(2,1)} %shard_map.37.x_ref), custom_call_target="tpu_custom_call" | custom-call | tf_op jit(solution)/shard_map/pallas_call | solution.py:358
